TPU v7x, 256 devices: a whole 4x4x8 slice. The times are simulated.
256 devices in a mesh: section: 16 (over z, x_hi), fsdp: 16 (over x_lo, y, core).
Axes of the slice: x: 4 (x_hi: 2, x_lo: 2; x = x_hi * 2 + x_lo), y: 4, z: 8, core: 2. Of those that a mesh axis runs over, the one named last changes fastest.
Arguments:
- x_fwd: bfloat16 [16, 384, 4096], P('section', None, 'fsdp'), may hold values from -6 to 6
- x_saved: bfloat16 [16, 384, 4096], P('section', None, 'fsdp'), may hold values from -6 to 6
- cotangent: bfloat16 [16, 384, 4096], P('section', None, 'fsdp'), may hold values from -6 to 6
- qkv_weight: bfloat16 [16, 4096, 3, 4096], P('section', None, None, 'fsdp')
- gain: float32 [16, 4096], P('section', 'fsdp'), may hold values from 0.1 to 1.9
- block_lists: int32 [8, 3, 2], replicated, may hold values from 0 to 2, as said below
- plan: int32 [16, 2], P('section'), may hold values from 0 to 7
Outputs:
- y_next: bfloat16 [16, 384, 4096], P('section', None, 'fsdp')
- dx_prev: bfloat16 [16, 384, 4096], P('section', None, 'fsdp')
- w_grad: bfloat16 [16, 4096, 3, 4096], P('section', None, None, 'fsdp')
- gain_grad: float32 [16, 4096], P('section', 'fsdp')
Inputs may be any that keep to these rules, and one draw needn't show every extreme that they name: block_lists[z, b, 0] = b; the 2 entries of a row are distinct.
All inputs are finite; a program needn't handle non-finite values.
Results may differ from a plain program's by a relative error of at most 0.024.
Values may be sent and summed in bfloat16 or wider, within the bound.
No kernel may reach another device: no remote copies, remote signals or barrier semaphores. Data moves between devices by JAX's collectives and lax.ppermute only.
A program may use at most 128 MiB of HBM per device.

v0:
```python
import math
import jax
import jax.numpy as jnp
from jax import lax
from jax.sharding import PartitionSpec as P

HD = 128
BLK = 128
EPS = 1e-05


def shifted(block, axis, distance):
    devices = range(lax.axis_size(axis))
    route = [((i - distance) % len(devices), i) for i in devices]
    return lax.ppermute(block, axis, route)


def attend(query, key_in, value, block_ids):
    tokens, feat_width = query.shape
    head_count = feat_width // HD
    block_count = tokens // BLK
    band_size = block_ids.shape[1]
    q_blocks = query.reshape(block_count, BLK, head_count, HD)
    k_rows = key_in.reshape(block_count, BLK, head_count, HD)[block_ids].reshape(
        block_count, band_size * BLK, head_count, HD
    )
    v_rows = value.reshape(block_count, BLK, head_count, HD)[block_ids].reshape(
        block_count, band_size * BLK, head_count, HD
    )
    scores = jnp.einsum("qthd,qshd->qhts", q_blocks, k_rows, preferred_element_type=jnp.float32) * (
        1.0 / math.sqrt(HD)
    )
    row_max = jnp.max(scores, axis=3, keepdims=True)
    expd = jnp.exp(scores - row_max)
    probs = expd / jnp.sum(expd, axis=3, keepdims=True)
    probs_low = probs.astype(jnp.bfloat16)
    output = jnp.einsum(
        "qhts,qshd->qthd", probs_low, v_rows, preferred_element_type=jnp.float32
    ).reshape(tokens, feat_width)
    return (output, (probs, probs_low, q_blocks, k_rows, v_rows))


def attend_back(upstream, block_ids, saved):
    probs, probs_low, q_blocks, k_rows, v_rows = saved
    block_count, block_len, head_count, head_size = q_blocks.shape
    band_size = block_ids.shape[1]
    tokens = block_count * block_len
    c_blocks = upstream.reshape(block_count, block_len, head_count, head_size)
    grad_vrows = jnp.einsum(
        "qhts,qthd->qshd", probs_low, c_blocks, preferred_element_type=jnp.float32
    )
    grad_p = jnp.einsum("qthd,qshd->qhts", c_blocks, v_rows, preferred_element_type=jnp.float32)
    grad_s = (
        probs * (grad_p - jnp.sum(probs * grad_p, axis=3, keepdims=True)) * (1.0 / math.sqrt(HD))
    )
    grad_s_low = grad_s.astype(jnp.bfloat16)
    grad_q = jnp.einsum("qhts,qshd->qthd", grad_s_low, k_rows, preferred_element_type=jnp.float32)
    grad_krows = jnp.einsum(
        "qhts,qthd->qshd", grad_s_low, q_blocks, preferred_element_type=jnp.float32
    )
    onehot = (
        block_ids[:, :, None] == jnp.arange(block_count, dtype=jnp.int32)[None, None, :]
    ).astype(jnp.float32)
    band_shape = (block_count, band_size, block_len, head_count, head_size)
    grad_k = jnp.einsum("qbk,qbthd->kthd", onehot, grad_krows.reshape(band_shape))
    grad_v = jnp.einsum("qbk,qbthd->kthd", onehot, grad_vrows.reshape(band_shape))
    return (grad_q.reshape(tokens, -1), grad_k.reshape(tokens, -1), grad_v.reshape(tokens, -1))


def on_device(x_fwd, x_saved, cotangent, qkv_weight, gain, block_lists, plan):
    forward_in = x_fwd[0]
    saved_in = x_saved[0]
    upstream = cotangent[0]
    weight = qkv_weight[0]
    gain_row = gain[0]
    full_width = weight.shape[0]
    local = weight.shape[2]
    tokens = forward_in.shape[0]
    w_flat = weight.reshape(full_width, 3 * local)
    lists_fwd = block_lists[plan[0, 0]]
    lists_bwd = block_lists[plan[0, 1]]
    wide_fwd = forward_in.astype(jnp.float32)
    wide_bwd = saved_in.astype(jnp.float32)
    scaled_fwd = (wide_fwd * gain_row[None, :]).astype(jnp.bfloat16)
    scaled_bwd = (wide_bwd * gain_row[None, :]).astype(jnp.bfloat16)
    sq_fwd, sq_bwd = lax.psum(
        (jnp.sum(wide_fwd * wide_fwd, axis=1), jnp.sum(wide_bwd * wide_bwd, axis=1)), "fsdp"
    )
    scale_fwd = lax.rsqrt(sq_fwd / full_width + EPS)
    scale_bwd = lax.rsqrt(sq_bwd / full_width + EPS)
    product_fwd = jnp.dot(
        lax.all_gather(scaled_fwd, "fsdp", axis=1, tiled=True),
        w_flat,
        preferred_element_type=jnp.float32,
    )
    whole_bwd = lax.all_gather(scaled_bwd, "fsdp", axis=1, tiled=True)
    product_bwd = jnp.dot(whole_bwd, w_flat, preferred_element_type=jnp.float32)
    proj_fwd = (scale_fwd[:, None] * product_fwd).astype(jnp.bfloat16)
    attn_fwd = attend(
        proj_fwd[:, :local], proj_fwd[:, local : 2 * local], proj_fwd[:, 2 * local :], lists_fwd
    )[0]
    result = (wide_fwd + attn_fwd).astype(jnp.bfloat16)
    sent_on = shifted(result[None], "section", 1)
    proj_bwd = (scale_bwd[:, None] * product_bwd).astype(jnp.bfloat16)
    saved = attend(
        proj_bwd[:, :local], proj_bwd[:, local : 2 * local], proj_bwd[:, 2 * local :], lists_bwd
    )[1]
    grad_q, grad_k, grad_v = attend_back(upstream, lists_bwd, saved)
    stacked = jnp.stack([grad_q, grad_k, grad_v], axis=1).reshape(tokens, 3 * local)
    grads = (scale_bwd[:, None] * stacked).astype(jnp.bfloat16)
    grad_w = lax.dot_general(
        whole_bwd, grads, (((0,), (0,)), ((), ())), preferred_element_type=jnp.float32
    )
    grad_w = grad_w.astype(jnp.bfloat16).reshape(1, full_width, 3, local)
    partial_in = lax.dot_general(
        grads, w_flat, (((1,), (1,)), ((), ())), preferred_element_type=jnp.float32
    )
    summed_in = lax.psum(partial_in.astype(jnp.bfloat16), "fsdp").astype(jnp.float32)
    own_in = lax.dynamic_slice_in_dim(summed_in, lax.axis_index("fsdp") * local, local, 1)
    row_total = jnp.sum(whole_bwd.astype(jnp.float32) * summed_in, axis=1)
    grad_x = upstream.astype(jnp.float32) + gain_row[None, :] * own_in
    grad_x = grad_x - (scale_bwd * scale_bwd * row_total / full_width)[:, None] * wide_bwd
    sent_back = shifted(grad_x.astype(jnp.bfloat16)[None], "section", -1)
    grad_gain = jnp.sum(wide_bwd * own_in, axis=0)[None]
    return (sent_on, sent_back, grad_w, grad_gain)


def solution(mesh):
    in_specs = (
        P("section", None, "fsdp"),
        P("section", None, "fsdp"),
        P("section", None, "fsdp"),
        P("section", None, None, "fsdp"),
        P("section", "fsdp"),
        P(),
        P("section", None),
    )
    out_specs = (
        P("section", None, "fsdp"),
        P("section", None, "fsdp"),
        P("section", None, None, "fsdp"),
        P("section", "fsdp"),
    )
    return jax.shard_map(
        on_device, mesh=mesh, in_specs=in_specs, out_specs=out_specs, check_vma=False
    )
```

profile of v0, /device:TPU:25, one launch (start us, length us, event | category | flops | bytes accessed | tf_op | source)
XLA Modules:
  0.0 275.0 jit_solution(14417627607529717031)
XLA Ops:
  7.2 1.9 fusion.21
  9.9 1.3 fusion.70
  13.7 8.7 %copy.55 = bf16[1,4096,3,256]{1,3,2,0:T(8,128)(2,1)} copy(bf16[1,4096,3,256]{3,1,2,0:T(8,128)(2,1)} %param.10) | data formatting | bytes 12582912 | tf_op args[3]
  24.1 26.6 %all-reduce = (f32[384]{0:T(512)S(1)}, f32[384]{0:T(512)S(1)}) all-reduce(f32[384]{0:T(512)S(1)} %get-tuple-element.28, f32[384]{0:T(512)S(1)} %get-tuple-element.32), channel_id=1, replica_groups=mesh['section'=16,'fsdp'=16] {'fsdp'}, use_global_device_ids=true, to_apply=%region_1.0 | all-reduce | flops 768 | bytes 6144 | tf_op jit(solution)/shard_map/psum | solution.py:86
  50.7 5.6 %all-gather.5.cloned.1.call-done = bf16[384,4096]{1,0:T(8,128)(2,1)} async-done(((bf16[384,256]{1,0:T(8,128)(2,1)}), bf16[384,4096]{1,0:T(8,128)(2,1)}) %all-gather.5.cloned.1.call-update) | async-done | bytes 3145744 | tf_op jit(solution)/shard_map/all_gather | solution.py:96
  56.3 6.4 %fusion.6 = bf16[384,768]{1,0:T(8,128)(2,1)S(1)} fusion(bf16[384,4096]{1,0:T(8,128)(2,1)} %all-gather.5.cloned.1.call-done, bf16[4096,768]{0,1:T(8,128)(2,1)} %bitcast.81, f32[384]{0:T(512)S(1)} %add_rsqrt_fusion), kind=kOutput, calls=%fused_computation.15 | convolution fusion | flops 2416508928 | bytes 10028544 | tf_op jit(solution)/shard_map/dot_general | solution.py:97
  64.8 1.3 fusion.76
  66.1 5.9 %convolution_bitcast_fusion.4 = f32[3,128,2,128]{1,3,2,0:T(8,128)S(1)} fusion(f32[3,2,128,256]{3,2,1,0:T(8,128)S(1)} %convolution_bitcast_fusion.1, bf16[3,256,2,128]{3,1,0,2:T(8,128)(2,1)S(1)} %bitcast.91, f32[3,2,128,256]{3,2,1,0:T(8,128)} %get-tuple-element.37, f32[3,2,128]{2,1,0:T(2,128)S(1)} %get-tuple-element.36), kind=kOutput, calls=%fused_computation.28 | convolution fusion | flops 51708928 | bytes 2362368 | tf_op jit(solution)/shard_map/qhts,qshd->qthd/dot_general | solution.py:57
  72.5 5.4 %convolution_bitcast_fusion = bf16[3,256,2,128]{1,3,2,0:T(8,128)(2,1)S(1)} fusion(bf16[3,128,2,128]{1,3,2,0:T(8,128)(2,1)S(1)} %copy.80, f32[3,2,128,256]{3,2,1,0:T(8,128)S(1)} %convolution_bitcast_fusion.1, f32[3,2,128,256]{3,2,1,0:T(8,128)} %get-tuple-element.37, f32[3,2,128]{2,1,0:T(2,128)S(1)} %get-tuple-element.36), kind=kOutput, calls=%fused_computation.21 | convolution fusion | flops 51708928 | bytes 2165760 | tf_op jit(solution)/shard_map/qhts,qthd->qshd/dot_general | solution.py:58
  78.0 0.7 copy.81
  79.8 1.7 fusion.32
  83.2 7.1 %convolution_convert_fusion.1 = bf16[384,4096]{1,0:T(8,128)(2,1)} fusion(bf16[384,768]{0,1:T(8,128)(2,1)S(1)} %bitcast.86, bf16[4096,768]{0,1:T(8,128)(2,1)} %bitcast.82), kind=kOutput, calls=%fused_computation.9 | convolution fusion | flops 2417491968 | bytes 10027008 | tf_op jit(solution)/shard_map/dot_general | solution.py:115
  90.9 11.8 %all-gather.3.cloned.1.call-done = bf16[384,4096]{1,0:T(8,128)(2,1)} async-done(((bf16[384,256]{1,0:T(8,128)(2,1)}), bf16[384,4096]{1,0:T(8,128)(2,1)}) %all-gather.3.cloned.1.call-update) | async-done | bytes 3145744 | tf_op jit(solution)/shard_map/all_gather | solution.py:92
  102.7 6.4 %fusion.5 = bf16[384,768]{1,0:T(8,128)(2,1)S(1)} fusion(bf16[384,4096]{1,0:T(8,128)(2,1)} %all-gather.3.cloned.1.call-done, bf16[4096,768]{0,1:T(8,128)(2,1)} %bitcast.83, f32[384]{0:T(512)S(1)} %add_rsqrt_fusion.1), kind=kOutput, calls=%fused_computation.14 | convolution fusion | flops 2416508928 | bytes 10028544 | tf_op jit(solution)/shard_map/dot_general | solution.py:91
  109.9 0.8 copy.59
  112.4 1.6 convolution_bitcast_fusion.5
  114.6 3.2 %collective-permute-start = (bf16[1,384,256]{2,1,0:T(8,128)(2,1)S(1)}, bf16[1,384,256]{2,1,0:T(8,128)(2,1)S(1)}, u32[]{:S(2)}, u32[]{:S(2)}) collective-permute-start(bf16[1,384,256]{2,1,0:T(8,128)(2,1)S(1)} %fusion.23), channel_id=1, source_target_pairs={{240,0},{0,16},{16,32},{32,48},{48,64},{64,80},{80,96},{96,112},{1... | collective-permute-start | bytes 589832 | tf_op jit(solution)/shard_map/ppermute | solution.py:15
  118.2 123.7 %all-reduce.3.cloned.1.call-done = bf16[384,4096]{1,0:T(8,128)(2,1)} async-done(((bf16[384,4096]{1,0:T(8,128)(2,1)}), bf16[384,4096]{1,0:T(8,128)(2,1)}) %all-reduce.3.cloned.1.call-update) | async-done | bytes 3145744 | tf_op jit(solution)/shard_map/psum | solution.py:118
  241.9 3.9 %multiply_reduce_fusion = f32[384]{0:T(512)S(1)} fusion(bf16[384,4096]{1,0:T(8,128)(2,1)} %all-gather.5.cloned.1.call-done, bf16[384,4096]{1,0:T(8,128)(2,1)} %all-reduce.3.cloned.1.call-done), kind=kLoop, calls=%fused_computation.8 | loop fusion | flops 6291072 | bytes 6292992 | tf_op jit(solution)/shard_map/reduce_sum | solution.py:120
  245.8 0.8 convert_element_type.94
  246.7 0.7 fusion.28
  247.4 5.4 %collective-permute-start.1 = (bf16[1,384,256]{2,1,0:T(8,128)(2,1)S(1)}, bf16[1,384,256]{2,1,0:T(8,128)(2,1)S(1)}, u32[]{:S(2)}, u32[]{:S(2)}) collective-permute-start(bf16[1,384,256]{2,1,0:T(8,128)(2,1)S(1)} %get-tuple-element.19), channel_id=1, source_target_pairs={{16,0},{32,16},{48,32},{64,48},{80,64},{96,80},{112,96},{128,112},... | collective-permute-start | bytes 589832 | tf_op jit(solution)/shard_map/ppermute | solution.py:15
  252.9 5.6 %convolution_convert_fusion = bf16[4096,768]{0,1:T(8,128)(2,1)} fusion(bf16[384,4096]{1,0:T(8,128)(2,1)S(1)} %copy-done.1, f32[384,768]{1,0:T(8,128)S(1)} %copy.89, f32[384]{0:T(512)S(1)} %add_rsqrt_fusion), kind=kOutput, calls=%fused_computation.7 | convolution fusion | flops 2419654656 | bytes 10618368 | tf_op jit(solution)/shard_map/dot_general | solution.py:111
  258.5 8.6 %copy.90 = bf16[1,4096,3,256]{3,1,2,0:T(8,128)(2,1)} copy(bf16[1,4096,3,256]{1,3,2,0:T(8,128)(2,1)} %bitcast.84) | data formatting | bytes 12582912
  (82 shorter events, 12.2 us)
Async XLA Ops:
  7.2 49.1 %all-gather.5.cloned.1.call-start = ((), (), s32[]{:S(2)}) async-start(), calls=%async_computation.1 | async-start | bytes 3342336 | tf_op jit(solution)/shard_map/all_gather | solution.py:96
  9.1 93.6 %all-gather.3.cloned.1.call-start = ((), (), s32[]{:S(2)}) async-start(), calls=%async_computation | async-start | bytes 3342336 | tf_op jit(solution)/shard_map/all_gather | solution.py:92
  9.8 232.1 %all-reduce.3.cloned.1.call-start = ((), (), s32[]{:S(2)}) async-start(), calls=%async_computation.2 | async-start | bytes 6291456 | tf_op jit(solution)/shard_map/psum | solution.py:118
  13.6 9.9 %copy-start.6 = (s32[8,3,2]{0,2,1:T(2,128)S(1)}, s32[8,3,2]{0,2,1:T(2,128)}, u32[]{:S(2)}) copy-start(s32[8,3,2]{0,2,1:T(2,128)} %param.12) | copy-start | bytes 580
  13.7 10.4 %copy-start.2 = (bf16[1,384,256]{2,1,0:T(8,128)(2,1)S(1)}, bf16[1,384,256]{2,1,0:T(8,128)(2,1)}, u32[]{:S(2)}) copy-start(bf16[1,384,256]{2,1,0:T(8,128)(2,1)} %param.9) | copy-start | bytes 589828
  111.4 1.0 copy-start.5
  111.9 2.6 copy-start.4
  114.6 152.4 %collective-permute-start = (bf16[1,384,256]{2,1,0:T(8,128)(2,1)S(1)}, bf16[1,384,256]{2,1,0:T(8,128)(2,1)S(1)}, u32[]{:S(2)}, u32[]{:S(2)}) collective-permute-start(bf16[1,384,256]{2,1,0:T(8,128)(2,1)S(1)} %fusion.23), channel_id=1, source_target_pairs={{240,0},{0,16},{16,32},{32,48},{48,64},{64,80},{80,96},{96,112},{1... | collective-permute-start | bytes 589832 | tf_op jit(solution)/shard_map/ppermute | solution.py:15
  241.9 3.9 %copy-start = (bf16[384,4096]{1,0:T(8,128)(2,1)S(1)}, bf16[384,4096]{1,0:T(8,128)(2,1)}, u32[]{:S(2)}) copy-start(bf16[384,4096]{1,0:T(8,128)(2,1)} %all-reduce.3.cloned.1.call-done) | copy-start | bytes 9437188
  245.8 0.9 copy-start.3
  245.8 0.9 copy-start.7
  245.8 7.1 %copy-start.1 = (bf16[384,4096]{1,0:T(8,128)(2,1)S(1)}, bf16[384,4096]{1,0:T(8,128)(2,1)}, u32[]{:S(2)}) copy-start(bf16[384,4096]{1,0:T(8,128)(2,1)} %all-gather.5.cloned.1.call-done) | copy-start | bytes 9437188
  247.4 19.6 %collective-permute-start.1 = (bf16[1,384,256]{2,1,0:T(8,128)(2,1)S(1)}, bf16[1,384,256]{2,1,0:T(8,128)(2,1)S(1)}, u32[]{:S(2)}, u32[]{:S(2)}) collective-permute-start(bf16[1,384,256]{2,1,0:T(8,128)(2,1)S(1)} %get-tuple-element.19), channel_id=1, source_target_pairs={{16,0},{32,16},{48,32},{64,48},{80,64},{96,80},{112,96},{128,112},... | collective-permute-start | bytes 589832 | tf_op jit(solution)/shard_map/ppermute | solution.py:15
Sparse Core Ops, SparseCore 0:
  10.3 45.9 all-gather.4
  58.7 44.0 all-gather.2
  105.4 136.4 all-reduce.2
where the time goes:
time: 276 us; the launch traced here: 275 us
  waiting for transfers between devices  142 us (51%)
  matrix products  43.6 us (16%)
  local copies, waits for them, and re-layouts  29 us (11%)
  blocking collectives  26.6 us (10%)
  between operations  17.8 us (6%)
  starting transfers between devices  8.75 us (3%)
  other arithmetic  7.41 us (3%)
    psum x1, waiting for transfers between devices, on_device(): lax.psum(partial_in.astype(jnp.bfloat16), 'fsdp').astype(jnp.float32)  124 us
    psum x1, blocking collectives, on_device(): lax.psum((jnp.sum(wide_fwd * wide_fwd, axis=1), jnp.sum(wide_bwd * wide_b...  26.6 us
    unnamed x22, local copies, waits for them, and re-layouts  19 us
    all_gather x1, waiting for transfers between devices, on_device(): lax.all_gather(scaled_fwd, 'fsdp', axis=1, tiled=True)  11.8 us
    ppermute x2, starting transfers between devices, shifted(): return lax.ppermute(block, axis, route)  8.63 us
    dot_general x1, matrix products, on_device(): lax.dot_general(grads, w_flat, (((1,), (1,)), ((), ())), preferred_elemen...  7.14 us
    dot_general x1, matrix products, on_device(): jnp.dot(lax.all_gather(scaled_fwd, 'fsdp', axis=1, tiled=True), w_flat, p...  6.37 us
    dot_general x1, matrix products, on_device(): product_bwd = jnp.dot(whole_bwd, w_flat, preferred_element_type=jnp.float32)  6.37 us
  transfers between devices with their start and end apart: 5, of which 3 were waited for; matrix products, arithmetic and copies ran while one was open for 28% of the time, Pallas kernels for 0%

commit v1 on v0

--- a/solution.py
+++ b/solution.py
@@ -93,7 +93,16 @@
         w_flat,
         preferred_element_type=jnp.float32,
     )
-    whole_bwd = lax.all_gather(scaled_bwd, "fsdp", axis=1, tiled=True)
+    map_the_group = lambda local_x: jnp.concatenate(
+        lax.all_to_all(
+            jnp.stack(lax.psum(1, axis_name="fsdp") * [local_x]),
+            axis_name="fsdp",
+            split_axis=0,
+            concat_axis=0,
+        ),
+        axis=1,
+    )
+    whole_bwd = map_the_group(scaled_bwd)
     product_bwd = jnp.dot(whole_bwd, w_flat, preferred_element_type=jnp.float32)
     proj_fwd = (scale_fwd[:, None] * product_fwd).astype(jnp.bfloat16)
     attn_fwd = attend(

time: 276 us -> 330 us (1.20)
  local copies, waits for them, and re-layouts: 29 us -> 76.5 us
  waiting for transfers between devices: 142 us -> 103 us
  blocking collectives: 26.6 us -> 49.7 us
  matrix products: 43.6 us -> 55.3 us
  starting transfers between devices: 8.75 us -> 13.9 us
  other arithmetic: 7.41 us -> 11.9 us
    psum x1, blocking collectives: 26.6 us -> 49.7 us  [on_device(): lax.psum((jnp.sum(wide_fwd * wide_fwd, axis=1), jnp.sum(wide_bwd * wide_b...]
    psum x1, waiting for transfers between devices: 124 us -> 103 us  [on_device(): lax.psum(partial_in.astype(jnp.bfloat16), 'fsdp').astype(jnp.float32)]
    all_gather x1, waiting for transfers between devices: 11.8 us -> 0.02 us  [on_device(): lax.all_gather(scaled_fwd, 'fsdp', axis=1, tiled=True)]
    all_to_all x0 -> x1, starting transfers between devices: none -> 6.09 us  [on_device(): lax.all_to_all(jnp.stack(lax.psum(1, axis_name='fsdp') * [local_x]), axis...]
    all_gather x1 -> x0, waiting for transfers between devices: 5.57 us -> none  [on_device(): whole_bwd = lax.all_gather(scaled_bwd, 'fsdp', axis=1, tiled=True)]
    unnamed x22 -> x46, local copies, waits for them, and re-layouts: 19 us -> 24.1 us
    gather x4, local copies, waits for them, and re-layouts: 1.3 us -> 6.23 us  [attend(): key_in.reshape(block_count, BLK, head_count, HD)[block_ids]]
    another operation x5 -> x3, local copies, waits for them, and re-layouts: 1.35 us -> 6.16 us  [on_device(): jnp.stack([grad_q, grad_k, grad_v], axis=1).reshape(tokens, 3 * local)]
  transfers between devices with their start and end apart: 5 -> 5, of which waited for: 3 -> 1; matrix products, arithmetic and copies ran while one was open for 28% -> 41% of each run, Pallas kernels for 0% -> 0%
where the time goes in v1:
time: 330 us; the launch traced here: 328 us
  waiting for transfers between devices  103 us (31%)
  local copies, waits for them, and re-layouts  76.5 us (23%)
  matrix products  55.3 us (17%)
  blocking collectives  49.7 us (15%)
  between operations  18.2 us (6%)
  starting transfers between devices  13.9 us (4%)
  other arithmetic  11.9 us (4%)
    psum x1, waiting for transfers between devices, on_device(): lax.psum(partial_in.astype(jnp.bfloat16), 'fsdp').astype(jnp.float32)  103 us
    psum x1, blocking collectives, on_device(): lax.psum((jnp.sum(wide_fwd * wide_fwd, axis=1), jnp.sum(wide_bwd * wide_b...  49.7 us
    unnamed x46, local copies, waits for them, and re-layouts  24.1 us
    ppermute x2, starting transfers between devices, shifted(): return lax.ppermute(block, axis, route)  7.75 us
    dot_general x1, matrix products, on_device(): lax.dot_general(grads, w_flat, (((1,), (1,)), ((), ())), preferred_elemen...  7.36 us
    dot_general x1, matrix products, attend_back(): jnp.einsum('qhts,qshd->qthd', grad_s_low, k_rows, preferred_element_type=...  7.36 us
    dot_general x1, matrix products, attend_back(): jnp.einsum('qhts,qthd->qshd', grad_s_low, q_blocks, preferred_element_typ...  6.69 us
  transfers between devices with their start and end apart: 5, of which 1 were waited for; matrix products, arithmetic and copies ran while one was open for 41% of the time, Pallas kernels for 0%

profile of v1, /device:TPU:25, one launch (start us, length us, event | category | flops | bytes accessed | tf_op | source)
XLA Modules:
  0.0 328.4 jit_solution(10628518043614622028)
XLA Ops:
  10.1 6.1 %all-to-all-start = ((bf16[16,384,256]{2,1,0:T(8,128)(2,1)}), bf16[16,384,256]{2,1,0:T(8,128)(2,1)S(1)}, u32[]{:S(2)}, u32[]{:S(2)}) async-start(bf16[16,384,256]{2,1,0:T(8,128)(2,1)} %stack.7), calls=%async_computation | async-start | bytes 6291456 | tf_op jit(solution)/shard_map/all_to_all | solution.py:97
  20.9 8.7 %copy.87 = bf16[1,4096,3,256]{1,3,2,0:T(8,128)(2,1)} copy(bf16[1,4096,3,256]{3,1,2,0:T(8,128)(2,1)} %param.10) | data formatting | bytes 12582912 | tf_op args[3]
  33.9 49.7 %all-reduce = (f32[384]{0:T(512)}, f32[384]{0:T(512)S(1)}) all-reduce(f32[384]{0:T(512)} %get-tuple-element.30, f32[384]{0:T(512)} %get-tuple-element.38), channel_id=1, replica_groups=mesh['section'=16,'fsdp'=16] {'fsdp'}, use_global_device_ids=true, to_apply=%region_1.0 | all-reduce | flops 768 | bytes 6144 | tf_op jit(solution)/shard_map/psum | solution.py:86
  85.3 2.4 copy.131
  89.0 2.7 fusion.6
  100.7 3.0 fusion.80
  103.7 3.7 %fusion.35 = bf16[3,2,256,128]{3,2,1,0:T(8,128)(2,1)} fusion(bf16[3,128,2,128]{3,2,1,0:T(2,128)(2,1)} %reshape_squeeze.7, f32[3,2,128]{2,1,0:T(2,128)} %get-tuple-element.36, bf16[3,128,2,128]{1,3,2,0:T(8,128)(2,1)} %copy.113, bf16[3,256,2,128]{3,1,0,2:T(8,128)(2,1)} %bitcast.112), kind=kOutput, calls=%fused_computation.58 | convolution fusion | flops 101450752 | bytes 1182720 | tf_op jit(solution)/shard_map/qhts,qthd->qshd/dot_general | solution.py:49
  110.0 2.1 stack_reshape.11
  116.1 2.1 convolution_bitcast_fusion.1
  118.2 6.7 %convolution_bitcast_fusion = bf16[3,256,2,128]{1,3,2,0:T(8,128)(2,1)} fusion(bf16[3,128,2,128]{1,3,2,0:T(8,128)(2,1)} %copy.113, f32[3,2,128,256]{3,2,1,0:T(8,128)} %convolution_bitcast_fusion.1, f32[3,2,128,256]{3,2,1,0:T(8,128)} %get-tuple-element.37, f32[3,2,128]{2,1,0:T(2,128)} %get-tuple-element.36), kind=kOutput, calls=%fused_computation.21 | convolution fusion | flops 51708928 | bytes 2165760 | tf_op jit(solution)/shard_map/qhts,qthd->qshd/dot_general | solution.py:58
  126.8 2.1 copy.114
  133.5 7.4 %convolution_bitcast_fusion.4 = f32[3,128,2,128]{1,3,2,0:T(8,128)} fusion(f32[3,2,128,256]{3,2,1,0:T(8,128)} %convolution_bitcast_fusion.1, bf16[3,256,2,128]{3,1,0,2:T(8,128)(2,1)} %bitcast.113, f32[3,2,128,256]{3,2,1,0:T(8,128)} %get-tuple-element.37, f32[3,2,128]{2,1,0:T(2,128)S(1)} %copy-done.20), kind=kOutput, calls=%fused_computation.28 | convolution fusion | flops 51708928 | bytes 2362368 | tf_op jit(solution)/shard_map/qhts,qshd->qthd/dot_general | solution.py:57
  144.8 2.2 fusion.13
  147.0 2.1 copy.120
  149.1 7.4 %convolution_convert_fusion.1 = bf16[384,4096]{1,0:T(8,128)(2,1)} fusion(bf16[384,768]{0,1:T(8,128)(2,1)} %bitcast.106, bf16[4096,768]{0,1:T(8,128)(2,1)} %bitcast.98), kind=kOutput, calls=%fused_computation.9 | convolution fusion | flops 2417491968 | bytes 10027008 | tf_op jit(solution)/shard_map/dot_general | solution.py:124
  157.4 6.4 %fusion.5 = bf16[384,768]{1,0:T(8,128)(2,1)S(1)} fusion(bf16[384,4096]{1,0:T(8,128)(2,1)} %all-gather.2.cloned.1.call-done, bf16[4096,768]{0,1:T(8,128)(2,1)} %bitcast.99, f32[384]{0:T(512)S(1)} %add_rsqrt_fusion.1), kind=kOutput, calls=%fused_computation.14 | convolution fusion | flops 2416508928 | bytes 10028544 | tf_op jit(solution)/shard_map/dot_general | solution.py:91
  178.3 2.3 convolution_multiply_fusion.3
  180.6 3.9 %convolution_bitcast_fusion.5 = f32[3,128,2,128]{1,3,2,0:T(8,128)} fusion(bf16[3,256,2,128]{3,1,0,2:T(8,128)(2,1)} %bitcast.114, f32[3,2,128]{2,1,0:T(2,128)S(1)} %fusion.75, f32[3,2,128,256]{3,2,1,0:T(8,128)} %convolution_multiply_fusion.3), kind=kOutput, calls=%fused_computation.29 | convolution fusion | flops 50922496 | bytes 1575936 | tf_op jit(solution)/shard_map/qhts,qshd->qthd/dot_general | solution.py:37
  190.2 2.3 collective-permute-start
  192.5 102.8 %all-reduce.3.cloned.1.call-done = bf16[384,4096]{1,0:T(8,128)(2,1)} async-done(((bf16[384,4096]{1,0:T(8,128)(2,1)}), bf16[384,4096]{1,0:T(8,128)(2,1)}) %all-reduce.3.cloned.1.call-update) | async-done | bytes 3145744 | tf_op jit(solution)/shard_map/psum | solution.py:127
  295.3 2.9 multiply_reduce_fusion
  299.9 5.4 %collective-permute-start.1 = (bf16[1,384,256]{2,1,0:T(8,128)(2,1)S(1)}, bf16[1,384,256]{2,1,0:T(8,128)(2,1)S(1)}, u32[]{:S(2)}, u32[]{:S(2)}) collective-permute-start(bf16[1,384,256]{2,1,0:T(8,128)(2,1)S(1)} %get-tuple-element.23), channel_id=1, source_target_pairs={{16,0},{32,16},{48,32},{64,48},{80,64},{96,80},{112,96},{128,112},... | collective-permute-start | bytes 589832 | tf_op jit(solution)/shard_map/ppermute | solution.py:15
  305.3 5.3 %convolution_convert_fusion = bf16[4096,768]{0,1:T(8,128)(2,1)} fusion(bf16[384,768]{0,1:T(8,128)(2,1)S(1)} %bitcast.107, bf16[384,4096]{1,0:T(8,128)(2,1)S(1)} %bitcast.103), kind=kOutput, calls=%fused_computation.7 | convolution fusion | flops 2419064832 | bytes 10027008 | tf_op jit(solution)/shard_map/dot_general | solution.py:120
  310.6 8.6 %copy.121 = bf16[1,4096,3,256]{3,1,2,0:T(8,128)(2,1)} copy(bf16[1,4096,3,256]{1,3,2,0:T(8,128)(2,1)} %bitcast.105) | data formatting | bytes 12582912
  (105 shorter events, 62.0 us)
Async XLA Ops:
  10.1 6.2 %copy-start.4 = (bf16[1,384,256]{2,1,0:T(8,128)(2,1)S(1)}, bf16[1,384,256]{2,1,0:T(8,128)(2,1)}, u32[]{:S(2)}) copy-start(bf16[1,384,256]{2,1,0:T(8,128)(2,1)} %param.8) | copy-start | bytes 589828
  10.1 6.2 %copy-start.8 = (bf16[1,384,256]{2,1,0:T(8,128)(2,1)S(1)}, bf16[1,384,256]{2,1,0:T(8,128)(2,1)}, u32[]{:S(2)}) copy-start(bf16[1,384,256]{2,1,0:T(8,128)(2,1)} %param.7) | copy-start | bytes 589828
  10.1 6.2 %copy-start.12 = (f32[1,256]{1,0:T(1,128)S(1)}, f32[1,256]{1,0:T(1,128)}, u32[]{:S(2)}) copy-start(f32[1,256]{1,0:T(1,128)} %param.11) | copy-start | bytes 3076
  10.1 7.6 %copy-start.19 = (s32[1,2]{1,0:T(1,128)S(1)}, s32[1,2]{1,0:T(1,128)}, u32[]{:S(2)}) copy-start(s32[1,2]{1,0:T(1,128)} %param.13) | copy-start | bytes 28
  10.1 73.5 %all-to-all-start = ((bf16[16,384,256]{2,1,0:T(8,128)(2,1)}), bf16[16,384,256]{2,1,0:T(8,128)(2,1)S(1)}, u32[]{:S(2)}, u32[]{:S(2)}) async-start(bf16[16,384,256]{2,1,0:T(8,128)(2,1)} %stack.7), calls=%async_computation | async-start | bytes 6291456 | tf_op jit(solution)/shard_map/all_to_all | solution.py:97
  16.2 141.1 %all-gather.2.cloned.1.call-start = ((), (), s32[]{:S(2)}) async-start(), calls=%async_computation.1 | async-start | bytes 3342336 | tf_op jit(solution)/shard_map/all_gather | solution.py:92
  17.7 277.6 %all-reduce.3.cloned.1.call-start = ((), (), s32[]{:S(2)}) async-start(), calls=%async_computation.2 | async-start | bytes 6291456 | tf_op jit(solution)/shard_map/psum | solution.py:127
  20.9 10.0 %copy-start.11 = (s32[8,3,2]{0,2,1:T(2,128)S(1)}, s32[8,3,2]{0,2,1:T(2,128)}, u32[]{:S(2)}) copy-start(s32[8,3,2]{0,2,1:T(2,128)} %param.12) | copy-start | bytes 580
  20.9 10.8 %copy-start.5 = (bf16[1,384,256]{2,1,0:T(8,128)(2,1)S(1)}, bf16[1,384,256]{2,1,0:T(8,128)(2,1)}, u32[]{:S(2)}) copy-start(bf16[1,384,256]{2,1,0:T(8,128)(2,1)} %param.9) | copy-start | bytes 589828
  31.1 2.8 copy-start.13
  83.6 8.1 %copy-start.15 = (f32[384]{0:T(512)}, f32[384]{0:T(512)S(1)}, u32[]{:S(2)}) copy-start(f32[384]{0:T(512)S(1)} %add_rsqrt_fusion) | copy-start | bytes 4612
  83.6 1.7 copy-start.1
  85.3 3.7 %copy-start = (bf16[1,4096,3,256]{1,3,2,0:T(8,128)(2,1)S(1)}, bf16[1,4096,3,256]{1,3,2,0:T(8,128)(2,1)}, u32[]{:S(2)}) copy-start(bf16[1,4096,3,256]{1,3,2,0:T(8,128)(2,1)} %copy.87) | copy-start | bytes 18874372
  99.0 8.4 %copy-start.14 = (s32[1,3,2]{1,2,0:T(2,128)S(1)}, s32[1,3,2]{1,2,0:T(2,128)}, u32[]{:S(2)}) copy-start(s32[1,3,2]{1,2,0:T(2,128)} %copy-done.13) | copy-start | bytes 76
  103.7 8.3 %copy-start.7 = (bf16[384,256]{1,0:T(8,128)(2,1)S(1)}, bf16[384,256]{1,0:T(8,128)(2,1)}, u32[]{:S(2)}) copy-start(bf16[384,256]{1,0:T(8,128)(2,1)} %get-tuple-element.24) | copy-start | bytes 589828
  124.9 8.6 %copy-start.20 = (f32[3,2,128]{2,1,0:T(2,128)S(1)}, f32[3,2,128]{2,1,0:T(2,128)}, u32[]{:S(2)}) copy-start(f32[3,2,128]{2,1,0:T(2,128)} %get-tuple-element.36) | copy-start | bytes 9220
  131.4 13.4 %copy-start.16 = (f32[384]{0:T(512)S(1)}, f32[384]{0:T(512)}, u32[]{:S(2)}) copy-start(f32[384]{0:T(512)} %copy-done.15) | copy-start | bytes 4612
  156.4 0.9 copy-start.18
  178.3 10.2 %copy-start.9 = (bf16[1,384,256]{2,1,0:T(8,128)(2,1)S(1)}, bf16[1,384,256]{2,1,0:T(8,128)(2,1)}, u32[]{:S(2)}) copy-start(bf16[1,384,256]{2,1,0:T(8,128)(2,1)} %param.7) | copy-start | bytes 589828
  190.2 129.1 %collective-permute-start = (bf16[1,384,256]{2,1,0:T(8,128)(2,1)}, bf16[1,384,256]{2,1,0:T(8,128)(2,1)}, u32[]{:S(2)}, u32[]{:S(2)}) collective-permute-start(bf16[1,384,256]{2,1,0:T(8,128)(2,1)} %fusion.26), channel_id=1, source_target_pairs={{240,0},{0,16},{16,32},{32,48},{48,64},{64,80},{80,96},{96,112},{1... | collective-permute-start | bytes 589832 | tf_op jit(solution)/shard_map/ppermute | solution.py:15
  295.3 2.9 copy-start.2
  298.3 0.9 copy-start.6
  298.3 7.1 %copy-start.3 = (bf16[384,3,256]{0,2,1:T(8,128)(2,1)S(1)}, bf16[384,3,256]{0,2,1:T(8,128)(2,1)}, u32[]{:S(2)}) copy-start(bf16[384,3,256]{0,2,1:T(8,128)(2,1)} %copy.120) | copy-start | bytes 1769476
  299.9 19.3 %collective-permute-start.1 = (bf16[1,384,256]{2,1,0:T(8,128)(2,1)S(1)}, bf16[1,384,256]{2,1,0:T(8,128)(2,1)S(1)}, u32[]{:S(2)}, u32[]{:S(2)}) collective-permute-start(bf16[1,384,256]{2,1,0:T(8,128)(2,1)S(1)} %get-tuple-element.23), channel_id=1, source_target_pairs={{16,0},{32,16},{48,32},{64,48},{80,64},{96,80},{112,96},{128,112},... | collective-permute-start | bytes 589832 | tf_op jit(solution)/shard_map/ppermute | solution.py:15
  (2 other events, 1.4 us)
Sparse Core Ops, SparseCore 0:
  19.4 62.5 all-gather.1
  156.6 138.6 all-reduce.2
